TPU v7x, 32 devices: a whole 2x2x4 slice. The times are simulated.
32 devices in a mesh: clips: 2 (over y), frame: 4 (over z), head: 2 (over x), seq: 2 (over core).
Axes of the slice: x: 2, y: 2, z: 4, core: 2. Of those that a mesh axis runs over, the one named last changes fastest.
Arguments:
- queries: bfloat16 [32, 1024, 1536], P(('clips', 'frame'), 'seq', 'head'), parts along dimension 0, may hold values from -150 to 150, as said below
- key_rows: bfloat16 [32, 1024, 1536], P(('clips', 'frame'), 'seq', 'head'), parts along dimension 0, may hold values from -5 to 5, as said below
- value_rows: bfloat16 [32, 1024, 1536], P(('clips', 'frame'), 'seq', 'head'), parts along dimension 0, may hold values from -6 to 6
- list_one: int32 [32, 2, 4], P('clips'), parts along dimension 0, may hold values from 0 to 7, as said below
- list_two: int32 [32, 2, 2], P('clips'), parts along dimension 0, may hold values from 0 to 7, as said below
- list_four: int32 [32, 2, 1], P('clips'), parts along dimension 0, may hold values from 0 to 7, as said below
- tile_counts: int32 [32, 2, 3], P('clips'), parts along dimension 0, may hold values from 0 to 4, as said below
Outputs:
- attended: bfloat16 [32, 1024, 1536], P(('clips', 'frame'), 'seq', 'head'), parts along dimension 0
There are 2 independent parts, one for each index of `clips`. A program takes and returns all parts, laid end to end along the dimension named above; each array names one. Nothing has to cross between parts.
Inputs may be any that keep to these rules, and one draw needn't show every extreme that they name: Real-valued queries; a few query rows of a frame may be far larger in magnitude than the others. `key_rows`: Real-valued keys of order one. The entries of list_one[f, e, :] are distinct tile numbers of the frame f - 1 (e = 0) or f + 1 (e = 1). The entries of list_two[f, e, :] are distinct tile numbers of the frame f - 2 (e = 0) or f + 2 (e = 1). The entries of list_four[f, e, :] are distinct tile numbers of the frame f - 4 (e = 0) or f + 4 (e = 1). tile_counts[f, e, j] counts the live leading entries of the list of distance 1, 2, 4 (j = 0, 1, 2) for frame f and direction e; it is 0 exactly where the source frame lies outside the clip, else at least 1 and at most that list's length; frame 0's lists toward later frames are full.
All inputs are finite; a program needn't handle non-finite values.
Results may differ from a plain program's by a relative error of at most 0.0032.
Values may be sent and summed in bfloat16 or wider, within the bound.
A program may use at most 128 MiB of HBM per device.

v0:
```python
import jax
import jax.numpy as jnp
from jax import lax
from jax.sharding import PartitionSpec as P

HEAD_DIM = 128
TILE_TOKENS = 128


def passed_along(block, axis, distance):
    devices = range(lax.axis_size(axis))
    route = [(i - distance, i) for i in devices if i - distance in devices]
    return lax.ppermute(block, axis, route)


def select_tiles(tile_array, sources, chosen):
    return tile_array[sources[:, None], chosen]


def to_tiles(rows):
    return rows.reshape(rows.shape[0], rows.shape[1] // TILE_TOKENS, TILE_TOKENS, rows.shape[2])


def pack_lists(tile_array, own_frames, local_index, reaches, frame_total):
    packed = {}
    for direction in (0, 1):
        step_sign = 2 * direction - 1
        for distance, tile_list in reaches:
            targets = jnp.clip(own_frames - step_sign * distance, 0, frame_total - 1)
            chosen = jnp.take(tile_list, targets, axis=0)[:, direction, :]
            packed[direction, distance] = select_tiles(tile_array, local_index, chosen)
    return packed


def join_lists(packed, from_later, from_earlier, frames_here):
    selected = {}
    for rank, distance in enumerate((1, 2, 4)):
        selected[1, distance] = jnp.concatenate(
            [packed[1, distance][distance:], from_later[rank]], axis=0
        )
        selected[0, distance] = jnp.concatenate(
            [from_earlier[rank], packed[0, distance][: frames_here - distance]], axis=0
        )
    return selected


def attend_frame(frame_item):
    query_block, pair_block, live_block = frame_item
    width = query_block.shape[1]
    score_scale = HEAD_DIM ** (-0.5)
    pieces = []
    for head_index in range(width // HEAD_DIM):
        column_start = head_index * HEAD_DIM
        query_head = query_block[:, column_start : column_start + HEAD_DIM]
        key_head = pair_block[:, column_start : column_start + HEAD_DIM]
        value_head = pair_block[:, width + column_start : width + column_start + HEAD_DIM]
        scores = (
            lax.dot_general(
                query_head, key_head, (((1,), (1,)), ((), ())), preferred_element_type=jnp.float32
            )
            * score_scale
        )
        scores = jnp.where(live_block[None, :] > 0, scores, -jnp.inf)
        row_max = jnp.max(scores, axis=1, keepdims=True)
        exponent = jnp.exp(scores - row_max)
        row_total = jnp.sum(exponent, axis=1, keepdims=True)
        rounded = exponent.astype(jnp.bfloat16)
        mixed_head = jnp.dot(rounded, value_head, preferred_element_type=jnp.float32) / row_total
        pieces.append(mixed_head)
    return jnp.concatenate(pieces, axis=1).astype(jnp.bfloat16)


def per_device(queries, key_rows, value_rows, list_one, list_two, list_four, tile_counts):
    frames_here = queries.shape[0]
    paired = jnp.concatenate([key_rows, value_rows], axis=2)
    channels = paired.shape[2]
    first_frame = lax.axis_index("frame") * frames_here
    local_index = jnp.arange(frames_here, dtype=jnp.int32)
    frame_total = list_one.shape[0]
    own_frames = first_frame + local_index
    own_counts = jnp.take(tile_counts, own_frames, axis=0)
    reaches = ((1, list_one), (2, list_two), (4, list_four))
    whole_frames = lax.all_gather(paired, "seq", axis=1, tiled=True)
    packed = pack_lists(to_tiles(whole_frames), own_frames, local_index, reaches, frame_total)
    from_later = passed_along((packed[1, 1][:1], packed[1, 2][:2], packed[1, 4]), "frame", -1)
    from_earlier = passed_along(
        (packed[0, 1][frames_here - 1 :], packed[0, 2][frames_here - 2 :], packed[0, 4]), "frame", 1
    )
    selected = join_lists(packed, from_later, from_earlier, frames_here)
    frame_length = whole_frames.shape[1]
    key_parts = [whole_frames]
    live_parts = [jnp.ones((frames_here, frame_length), jnp.int32)]
    for direction in (0, 1):
        for slot_index, (distance, tile_list) in enumerate(reaches):
            tile_group = selected[direction, distance]
            length = tile_group.shape[1]
            key_parts.append(tile_group.reshape(frames_here, length * TILE_TOKENS, channels))
            slot_rank = jnp.arange(length * TILE_TOKENS, dtype=jnp.int32) // TILE_TOKENS
            live_parts.append(
                (slot_rank[None, :] < own_counts[:, direction, slot_index][:, None]).astype(
                    jnp.int32
                )
            )
    key_set = jnp.concatenate(key_parts, axis=1)
    live_slots = jnp.concatenate(live_parts, axis=1)
    return lax.map(attend_frame, (queries, key_set, live_slots))


def solution(mesh):
    placed = (
        P(("clips", "frame"), "seq", "head"),
        P(("clips", "frame"), "seq", "head"),
        P(("clips", "frame"), "seq", "head"),
        P("clips", None, None),
        P("clips", None, None),
        P("clips", None, None),
        P("clips", None, None),
    )
    return jax.shard_map(
        per_device,
        mesh=mesh,
        in_specs=placed,
        out_specs=P(("clips", "frame"), "seq", "head"),
        check_vma=False,
    )
```

profile of v0, /device:TPU:7, one launch (start us, length us, event | category | flops | bytes accessed | tf_op | source)
XLA Modules:
  0.0 473.4 jit_solution(3644444854377102763)
XLA Ops:
  6.5 6.0 %pad_maximum_fusion = bf16[4,512,1536]{2,1,0:T(8,128)(2,1)} fusion(bf16[4,512,768]{2,1,0:T(8,128)(2,1)} %param.17, bf16[4,512,768]{2,1,0:T(8,128)(2,1)} %param.16), kind=kLoop, calls=%fused_computation.119 | loop fusion | flops 12582912 | bytes 12582912 | tf_op jit(solution)/shard_map/concatenate | solution.py:75
  20.2 18.8 %all-gather.2.cloned.1.call-done = bf16[4,1024,1536]{2,1,0:T(8,128)(2,1)} async-done(((bf16[4,512,1536]{2,1,0:T(8,128)(2,1)}), bf16[4,1024,1536]{2,1,0:T(8,128)(2,1)}) %all-gather.2.cloned.1.call-update) | async-done | bytes 12582928 | tf_op jit(solution)/shard_map/all_gather | solution.py:83
  39.1 8.2 %gather_fusion.1 = bf16[16,128,1536]{2,1,0:T(8,128)(2,1)} fusion(bf16[4,8,128,1536]{3,2,1,0:T(8,128)(2,1)} %bitcast.97, s32[16]{0:T(128)S(1)} %reshape.429), kind=kCustom, calls=%fused_computation.7 | custom fusion | bytes 12583040 | tf_op jit(solution)/shard_map/gather | solution.py:17
  54.7 8.1 %gather_fusion.4 = bf16[16,128,1536]{2,1,0:T(8,128)(2,1)} fusion(bf16[4,8,128,1536]{3,2,1,0:T(8,128)(2,1)} %bitcast.98, s32[16]{0:T(128)S(1)} %reshape.449), kind=kCustom, calls=%fused_computation.10 | custom fusion | bytes 12583040 | tf_op jit(solution)/shard_map/gather | solution.py:17
  81.5 6.4 %gather_fusion.3 = bf16[4,128,1536]{2,1,0:T(8,128)(2,1)} fusion(bf16[4,8,128,1536]{3,2,1,0:T(8,128)(2,1)} %bitcast.100, s32[4]{0:T(128)S(1)} %or_bitcast_fusion.1), kind=kCustom, calls=%fused_computation.9 | custom fusion | bytes 3145760 | tf_op jit(solution)/shard_map/gather | solution.py:17
  92.4 5.3 %gather_fusion.5 = bf16[8,128,1536]{2,1,0:T(8,128)(2,1)S(1)} fusion(bf16[4,8,128,1536]{3,2,1,0:T(8,128)(2,1)} %bitcast.101, s32[8]{0:T(128)S(1)} %reshape.455), kind=kCustom, calls=%fused_computation.11 | custom fusion | bytes 6291520 | tf_op jit(solution)/shard_map/gather | solution.py:17
  101.0 10.5 %constant_dynamic-update-slice_fusion.12 = bf16[4,2816,1536]{2,1,0:T(8,128)(2,1)} fusion(bf16[4,1024,1536]{2,1,0:T(8,128)(2,1)} %all-gather.2.cloned.1.call-done), kind=kLoop, calls=%fused_computation.139 | loop fusion | bytes 25165824
  121.6 15.9 %collective-permute-done.1 = bf16[2,2,128,1536]{3,2,1,0:T(8,128)(2,1)} collective-permute-done((bf16[2,2,128,1536]{3,2,1,0:T(8,128)(2,1)}, bf16[2,2,128,1536]{3,2,1,0:T(8,128)(2,1)}, u32[]{:S(2)}, u32[]{:S(2)}) %collective-permute-start.1) | collective-permute-done | bytes 1572896 | tf_op jit(solution)/shard_map/ppermute | solution.py:13
  147.8 14.0 %collective-permute-done.4 = bf16[2,2,128,1536]{3,2,1,0:T(8,128)(2,1)S(1)} collective-permute-done((bf16[2,2,128,1536]{3,2,1,0:T(8,128)(2,1)}, bf16[2,2,128,1536]{3,2,1,0:T(8,128)(2,1)S(1)}, u32[]{:S(2)}, u32[]{:S(2)}) %collective-permute-start.4) | collective-permute-done | bytes 1572896 | tf_op jit(solution)/shard_map/ppermute | solution.py:13
  162.1 9.1 %collective-permute-done.2 = bf16[4,1,128,1536]{3,2,0,1:T(8,128)(2,1)} collective-permute-done((bf16[4,1,128,1536]{3,2,0,1:T(8,128)(2,1)}, bf16[4,1,128,1536]{3,2,0,1:T(8,128)(2,1)}, u32[]{:S(2)}, u32[]{:S(2)}) %collective-permute-start.2) | collective-permute-done | bytes 1572896 | tf_op jit(solution)/shard_map/ppermute | solution.py:13
  178.8 16.7 %collective-permute-done.5 = bf16[4,1,128,1536]{3,2,0,1:T(8,128)(2,1)S(1)} collective-permute-done((bf16[4,1,128,1536]{3,2,0,1:T(8,128)(2,1)S(1)}, bf16[4,1,128,1536]{3,2,0,1:T(8,128)(2,1)S(1)}, u32[]{:S(2)}, u32[]{:S(2)}) %collective-permute-start.5) | collective-permute-done | bytes 1572896 | tf_op jit(solution)/shard_map/ppermute | solution.py:13
  196.8 269.8 %while.10 = (s32[]{:T(128)}, bf16[4,512,768]{2,1,0:T(8,128)(2,1)}, s32[4,2816]{1,0:T(4,128)S(1)}, bf16[4,512,768]{2,1,0:T(8,128)(2,1)}, bf16[4,2816,1536]{2,1,0:T(8,128)(2,1)}, /*index=5*/s32[]{:T(128)}) while((s32[]{:T(128)}, bf16[4,512,768]{2,1,0:T(8,128)(2,1)}, s32[4,2816]{1,0:T(4,128)S(1)}, bf16[4,512,768]{2,1,0:T(8,128)(2,1)}, ...), condition=%wide.region_13.17_spmd, body=%wide.region_0.16_spmd.sunk | while | flops 4525126656 | bytes 196972000 | solution.py:106
  196.8 7.4 %dynamic-slice_bitcast_fusion.4 = bf16[2816,1536]{1,0:T(8,128)(2,1)} fusion(bf16[4,2816,1536]{2,1,0:T(8,128)(2,1)} %get-tuple-element.159, s32[]{:T(128)} %get-tuple-element.149), kind=kLoop, calls=%fused_computation.13.clone.1 | loop fusion | bytes 17301508 | tf_op jit(solution)/shard_map/while/body/jit(dynamic_index_in_dim)/squeeze | solution.py:106
  221.6 10.9 %fusion.220 = (f32[512]{0:T(512)S(1)}, f32[512]{0:T(512)S(1)}, f32[512]{0:T(512)S(1)}, f32[512]{0:T(512)S(1)}, f32[512]{0:T(512)S(1)}, /*index=5*/f32[512]{0:T(512)S(1)}, f32[512,2816]{1,0:T(8,128)}) fusion(f32[512,2816]{1,0:T(8,128)} %get-tuple-element.130, f32[512]{0:T(512)S(1)} %get-tuple-element.131, ...), kind=kOutput, calls=%fused_computation.42.clone.1 | convolution fusion | flops 397931520 | bytes 35474176 | tf_op jit(solution)/shard_map/while/body/eval_jaxpr/dot_general | solution.py:58
  232.5 8.0 %fusion.222 = (f32[512]{0:T(512)S(1)}, f32[512]{0:T(512)S(1)}, f32[512]{0:T(512)S(1)}, f32[512]{0:T(512)S(1)}) fusion(f32[512,2816]{1,0:T(8,128)S(1)} %fusion.219, f32[512]{0:T(512)S(1)} %get-tuple-element.135, pred[2816]{0:T(1024)(128)(4,1)S(1)} %compare_reduce_fusion.2, f32[512]{0:T(512)S(1)} %get-tuple-element.134, ...), kind=kLoop, calls=%fused_computation.40.clone.1 | loop fusion | flops 23066624 | bytes 23087872 | tf_op jit(solution)/shard_map/while/body/eval_jaxpr/reduce_sum | solution.py:66
  264.2 7.4 %dynamic-slice_bitcast_fusion.4 = bf16[2816,1536]{1,0:T(8,128)(2,1)} fusion(bf16[4,2816,1536]{2,1,0:T(8,128)(2,1)} %get-tuple-element.159, s32[]{:T(128)} %get-tuple-element.149), kind=kLoop, calls=%fused_computation.13.clone.1 | loop fusion | bytes 17301508 | tf_op jit(solution)/shard_map/while/body/jit(dynamic_index_in_dim)/squeeze | solution.py:106
  289.0 10.9 %fusion.220 = (f32[512]{0:T(512)S(1)}, f32[512]{0:T(512)S(1)}, f32[512]{0:T(512)S(1)}, f32[512]{0:T(512)S(1)}, f32[512]{0:T(512)S(1)}, /*index=5*/f32[512]{0:T(512)S(1)}, f32[512,2816]{1,0:T(8,128)}) fusion(f32[512,2816]{1,0:T(8,128)} %get-tuple-element.130, f32[512]{0:T(512)S(1)} %get-tuple-element.131, ...), kind=kOutput, calls=%fused_computation.42.clone.1 | convolution fusion | flops 397931520 | bytes 35474176 | tf_op jit(solution)/shard_map/while/body/eval_jaxpr/dot_general | solution.py:58
  299.9 8.0 %fusion.222 = (f32[512]{0:T(512)S(1)}, f32[512]{0:T(512)S(1)}, f32[512]{0:T(512)S(1)}, f32[512]{0:T(512)S(1)}) fusion(f32[512,2816]{1,0:T(8,128)S(1)} %fusion.219, f32[512]{0:T(512)S(1)} %get-tuple-element.135, pred[2816]{0:T(1024)(128)(4,1)S(1)} %compare_reduce_fusion.2, f32[512]{0:T(512)S(1)} %get-tuple-element.134, ...), kind=kLoop, calls=%fused_computation.40.clone.1 | loop fusion | flops 23066624 | bytes 23087872 | tf_op jit(solution)/shard_map/while/body/eval_jaxpr/reduce_sum | solution.py:66
  331.7 7.4 %dynamic-slice_bitcast_fusion.4 = bf16[2816,1536]{1,0:T(8,128)(2,1)} fusion(bf16[4,2816,1536]{2,1,0:T(8,128)(2,1)} %get-tuple-element.159, s32[]{:T(128)} %get-tuple-element.149), kind=kLoop, calls=%fused_computation.13.clone.1 | loop fusion | bytes 17301508 | tf_op jit(solution)/shard_map/while/body/jit(dynamic_index_in_dim)/squeeze | solution.py:106
  356.5 10.9 %fusion.220 = (f32[512]{0:T(512)S(1)}, f32[512]{0:T(512)S(1)}, f32[512]{0:T(512)S(1)}, f32[512]{0:T(512)S(1)}, f32[512]{0:T(512)S(1)}, /*index=5*/f32[512]{0:T(512)S(1)}, f32[512,2816]{1,0:T(8,128)}) fusion(f32[512,2816]{1,0:T(8,128)} %get-tuple-element.130, f32[512]{0:T(512)S(1)} %get-tuple-element.131, ...), kind=kOutput, calls=%fused_computation.42.clone.1 | convolution fusion | flops 397931520 | bytes 35474176 | tf_op jit(solution)/shard_map/while/body/eval_jaxpr/dot_general | solution.py:58
  367.4 8.0 %fusion.222 = (f32[512]{0:T(512)S(1)}, f32[512]{0:T(512)S(1)}, f32[512]{0:T(512)S(1)}, f32[512]{0:T(512)S(1)}) fusion(f32[512,2816]{1,0:T(8,128)S(1)} %fusion.219, f32[512]{0:T(512)S(1)} %get-tuple-element.135, pred[2816]{0:T(1024)(128)(4,1)S(1)} %compare_reduce_fusion.2, f32[512]{0:T(512)S(1)} %get-tuple-element.134, ...), kind=kLoop, calls=%fused_computation.40.clone.1 | loop fusion | flops 23066624 | bytes 23087872 | tf_op jit(solution)/shard_map/while/body/eval_jaxpr/reduce_sum | solution.py:66
  399.1 7.4 %dynamic-slice_bitcast_fusion.4 = bf16[2816,1536]{1,0:T(8,128)(2,1)} fusion(bf16[4,2816,1536]{2,1,0:T(8,128)(2,1)} %get-tuple-element.159, s32[]{:T(128)} %get-tuple-element.149), kind=kLoop, calls=%fused_computation.13.clone.1 | loop fusion | bytes 17301508 | tf_op jit(solution)/shard_map/while/body/jit(dynamic_index_in_dim)/squeeze | solution.py:106
  424.0 10.9 %fusion.220 = (f32[512]{0:T(512)S(1)}, f32[512]{0:T(512)S(1)}, f32[512]{0:T(512)S(1)}, f32[512]{0:T(512)S(1)}, f32[512]{0:T(512)S(1)}, /*index=5*/f32[512]{0:T(512)S(1)}, f32[512,2816]{1,0:T(8,128)}) fusion(f32[512,2816]{1,0:T(8,128)} %get-tuple-element.130, f32[512]{0:T(512)S(1)} %get-tuple-element.131, ...), kind=kOutput, calls=%fused_computation.42.clone.1 | convolution fusion | flops 397931520 | bytes 35474176 | tf_op jit(solution)/shard_map/while/body/eval_jaxpr/dot_general | solution.py:58
  434.8 8.0 %fusion.222 = (f32[512]{0:T(512)S(1)}, f32[512]{0:T(512)S(1)}, f32[512]{0:T(512)S(1)}, f32[512]{0:T(512)S(1)}) fusion(f32[512,2816]{1,0:T(8,128)S(1)} %fusion.219, f32[512]{0:T(512)S(1)} %get-tuple-element.135, pred[2816]{0:T(1024)(128)(4,1)S(1)} %compare_reduce_fusion.2, f32[512]{0:T(512)S(1)} %get-tuple-element.134, ...), kind=kLoop, calls=%fused_computation.40.clone.1 | loop fusion | flops 23066624 | bytes 23087872 | tf_op jit(solution)/shard_map/while/body/eval_jaxpr/reduce_sum | solution.py:66
  (216 shorter events, 235.2 us)
Async XLA Ops:
  6.5 32.5 %all-gather.2.cloned.1.call-start = ((), (), s32[]{:S(2)}) async-start(), calls=%async_computation | async-start | bytes 18874368 | tf_op jit(solution)/shard_map/all_gather | solution.py:83
  66.8 49.9 %collective-permute-start = (bf16[1,4,128,1536]{3,2,1,0:T(8,128)(2,1)}, bf16[1,4,128,1536]{3,2,1,0:T(8,128)(2,1)}, u32[]{:S(2)}, u32[]{:S(2)}) collective-permute-start(bf16[1,4,128,1536]{3,2,1,0:T(8,128)(2,1)} %slice_bitcast_fusion.1), channel_id=1, source_target_pairs={{0,4},{4,8},{8,12},{1,5},{5,9},{9,13},{2,6},{6,10},{10,14},{3,7},{... | collective-permute-start | bytes 4718600 | tf_op jit(solution)/shard_map/ppermute | solution.py:13
  78.4 59.1 %collective-permute-start.1 = (bf16[2,2,128,1536]{3,2,1,0:T(8,128)(2,1)}, bf16[2,2,128,1536]{3,2,1,0:T(8,128)(2,1)}, u32[]{:S(2)}, u32[]{:S(2)}) collective-permute-start(bf16[2,2,128,1536]{3,2,1,0:T(8,128)(2,1)} %bitcast.15), channel_id=1, source_target_pairs={{0,4},{4,8},{8,12},{1,5},{5,9},{9,13},{2,6},{6,10},{10,14},{3,7},{... | collective-permute-start | bytes 4718600 | tf_op jit(solution)/shard_map/ppermute | solution.py:13
  87.9 83.2 %collective-permute-start.2 = (bf16[4,1,128,1536]{3,2,0,1:T(8,128)(2,1)}, bf16[4,1,128,1536]{3,2,0,1:T(8,128)(2,1)}, u32[]{:S(2)}, u32[]{:S(2)}) collective-permute-start(bf16[4,1,128,1536]{3,2,0,1:T(8,128)(2,1)} %bitcast.22), channel_id=1, source_target_pairs={{0,4},{4,8},{8,12},{1,5},{5,9},{9,13},{2,6},{6,10},{10,14},{3,7},{... | collective-permute-start | bytes 4718600 | tf_op jit(solution)/shard_map/ppermute | solution.py:13
  91.1 53.0 %collective-permute-start.3 = (bf16[1,4,128,1536]{3,2,1,0:T(8,128)(2,1)}, bf16[1,4,128,1536]{3,2,1,0:T(8,128)(2,1)}, u32[]{:S(2)}, u32[]{:S(2)}) collective-permute-start(bf16[1,4,128,1536]{3,2,1,0:T(8,128)(2,1)} %slice_bitcast_fusion), channel_id=1, source_target_pairs={{4,0},{8,4},{12,8},{5,1},{9,5},{13,9},{6,2},{10,6},{14,10},{7,3},{... | collective-permute-start | bytes 4718600 | tf_op jit(solution)/shard_map/ppermute | solution.py:13
  99.7 62.1 %collective-permute-start.4 = (bf16[2,2,128,1536]{3,2,1,0:T(8,128)(2,1)}, bf16[2,2,128,1536]{3,2,1,0:T(8,128)(2,1)S(1)}, u32[]{:S(2)}, u32[]{:S(2)}) collective-permute-start(bf16[2,2,128,1536]{3,2,1,0:T(8,128)(2,1)} %bitcast.30), channel_id=1, source_target_pairs={{4,0},{8,4},{12,8},{5,1},{9,5},{13,9},{6,2},{10,6},{14,10},{7,3},{... | collective-permute-start | bytes 4718600 | tf_op jit(solution)/shard_map/ppermute | solution.py:13
  116.8 78.7 %collective-permute-start.5 = (bf16[4,1,128,1536]{3,2,0,1:T(8,128)(2,1)S(1)}, bf16[4,1,128,1536]{3,2,0,1:T(8,128)(2,1)S(1)}, u32[]{:S(2)}, u32[]{:S(2)}) collective-permute-start(bf16[4,1,128,1536]{3,2,0,1:T(8,128)(2,1)S(1)} %bitcast.111), channel_id=1, source_target_pairs={{4,0},{8,4},{12,8},{5,1},{9,5},{13,9},{6,2},{10,6},{14,10},{7,3},{... | collective-permute-start | bytes 4718600 | tf_op jit(solution)/shard_map/ppermute | solution.py:13
  118.1 19.4 %copy-start.3 = (bf16[4,128,1536]{2,1,0:T(8,128)(2,1)S(1)}, bf16[4,128,1536]{2,1,0:T(8,128)(2,1)}, u32[]{:S(2)}) copy-start(bf16[4,128,1536]{2,1,0:T(8,128)(2,1)} %get-tuple-element.69) | copy-start | bytes 4718596
  145.7 16.1 %copy-start.2 = (bf16[4,128,1536]{2,1,0:T(8,128)(2,1)S(1)}, bf16[4,128,1536]{2,1,0:T(8,128)(2,1)}, u32[]{:S(2)}) copy-start(bf16[4,128,1536]{2,1,0:T(8,128)(2,1)} %get-tuple-element.66) | copy-start | bytes 4718596
  205.3 14.2 %copy-start = (bf16[512,768]{1,0:T(8,128)(2,1)}, bf16[512,768]{1,0:T(8,128)(2,1)S(1)}, u32[]{:S(2)}) copy-start(bf16[512,768]{1,0:T(8,128)(2,1)S(1)} %dynamic-slice_bitcast_fusion.5) | copy-start | bytes 2359300 | tf_op jit(solution)/shard_map/while
  232.5 11.3 %slice-start.2 = ((s8[5767168]{0:T(1024)(128)(4,1)}), s8[4194304]{0:T(1024)(128)(4,1)S(1)}, s32[]{:S(2)}) async-start(s8[5767168]{0:T(1024)(128)(4,1)} %bitcast.95), calls=%async_computation.3 | async-start | bytes 8388608 | tf_op jit(solution)/shard_map/while
  232.5 11.3 %slice-start.3 = ((s8[5767168]{0:T(1024)(128)(4,1)}), s8[1572864]{0:T(1024)(128)(4,1)S(1)}, s32[]{:S(2)}) async-start(s8[5767168]{0:T(1024)(128)(4,1)} %bitcast.95), calls=%async_computation.4 | async-start | bytes 3145728 | tf_op jit(solution)/shard_map/while
  251.9 6.7 %slice-start = ((s8[5767168]{0:T(1024)(128)(4,1)}), s8[4194304]{0:T(1024)(128)(4,1)S(1)}, s32[]{:S(2)}) async-start(s8[5767168]{0:T(1024)(128)(4,1)} %bitcast.93), calls=%async_computation.1 | async-start | bytes 8388608 | tf_op jit(solution)/shard_map/while
  272.8 14.2 %copy-start = (bf16[512,768]{1,0:T(8,128)(2,1)}, bf16[512,768]{1,0:T(8,128)(2,1)S(1)}, u32[]{:S(2)}) copy-start(bf16[512,768]{1,0:T(8,128)(2,1)S(1)} %dynamic-slice_bitcast_fusion.5) | copy-start | bytes 2359300 | tf_op jit(solution)/shard_map/while
  299.9 11.3 %slice-start.2 = ((s8[5767168]{0:T(1024)(128)(4,1)}), s8[4194304]{0:T(1024)(128)(4,1)S(1)}, s32[]{:S(2)}) async-start(s8[5767168]{0:T(1024)(128)(4,1)} %bitcast.95), calls=%async_computation.3 | async-start | bytes 8388608 | tf_op jit(solution)/shard_map/while
  299.9 11.3 %slice-start.3 = ((s8[5767168]{0:T(1024)(128)(4,1)}), s8[1572864]{0:T(1024)(128)(4,1)S(1)}, s32[]{:S(2)}) async-start(s8[5767168]{0:T(1024)(128)(4,1)} %bitcast.95), calls=%async_computation.4 | async-start | bytes 3145728 | tf_op jit(solution)/shard_map/while
  319.4 6.7 %slice-start = ((s8[5767168]{0:T(1024)(128)(4,1)}), s8[4194304]{0:T(1024)(128)(4,1)S(1)}, s32[]{:S(2)}) async-start(s8[5767168]{0:T(1024)(128)(4,1)} %bitcast.93), calls=%async_computation.1 | async-start | bytes 8388608 | tf_op jit(solution)/shard_map/while
  340.3 14.2 %copy-start = (bf16[512,768]{1,0:T(8,128)(2,1)}, bf16[512,768]{1,0:T(8,128)(2,1)S(1)}, u32[]{:S(2)}) copy-start(bf16[512,768]{1,0:T(8,128)(2,1)S(1)} %dynamic-slice_bitcast_fusion.5) | copy-start | bytes 2359300 | tf_op jit(solution)/shard_map/while
  367.4 11.3 %slice-start.2 = ((s8[5767168]{0:T(1024)(128)(4,1)}), s8[4194304]{0:T(1024)(128)(4,1)S(1)}, s32[]{:S(2)}) async-start(s8[5767168]{0:T(1024)(128)(4,1)} %bitcast.95), calls=%async_computation.3 | async-start | bytes 8388608 | tf_op jit(solution)/shard_map/while
  367.4 11.3 %slice-start.3 = ((s8[5767168]{0:T(1024)(128)(4,1)}), s8[1572864]{0:T(1024)(128)(4,1)S(1)}, s32[]{:S(2)}) async-start(s8[5767168]{0:T(1024)(128)(4,1)} %bitcast.95), calls=%async_computation.4 | async-start | bytes 3145728 | tf_op jit(solution)/shard_map/while
  386.8 6.7 %slice-start = ((s8[5767168]{0:T(1024)(128)(4,1)}), s8[4194304]{0:T(1024)(128)(4,1)S(1)}, s32[]{:S(2)}) async-start(s8[5767168]{0:T(1024)(128)(4,1)} %bitcast.93), calls=%async_computation.1 | async-start | bytes 8388608 | tf_op jit(solution)/shard_map/while
  407.7 14.2 %copy-start = (bf16[512,768]{1,0:T(8,128)(2,1)}, bf16[512,768]{1,0:T(8,128)(2,1)S(1)}, u32[]{:S(2)}) copy-start(bf16[512,768]{1,0:T(8,128)(2,1)S(1)} %dynamic-slice_bitcast_fusion.5) | copy-start | bytes 2359300 | tf_op jit(solution)/shard_map/while
  434.8 11.3 %slice-start.2 = ((s8[5767168]{0:T(1024)(128)(4,1)}), s8[4194304]{0:T(1024)(128)(4,1)S(1)}, s32[]{:S(2)}) async-start(s8[5767168]{0:T(1024)(128)(4,1)} %bitcast.95), calls=%async_computation.3 | async-start | bytes 8388608 | tf_op jit(solution)/shard_map/while
  434.8 11.3 %slice-start.3 = ((s8[5767168]{0:T(1024)(128)(4,1)}), s8[1572864]{0:T(1024)(128)(4,1)S(1)}, s32[]{:S(2)}) async-start(s8[5767168]{0:T(1024)(128)(4,1)} %bitcast.95), calls=%async_computation.4 | async-start | bytes 3145728 | tf_op jit(solution)/shard_map/while
  (11 other events, 37.0 us)
Sparse Core Ops, SparseCore 0:
  12.7 26.3 all-gather.1
where the time goes:
time: 479 us; the launch traced here: 473 us
  matrix products  194 us (41%)
  local copies, waits for them, and re-layouts  130 us (27%)
  waiting for transfers between devices  74.6 us (16%)
  other arithmetic  46.9 us (10%)
  starting transfers between devices  14.4 us (3%)
  between operations  13.6 us (3%)
    dot_general x24, matrix products, attend_frame(): lax.dot_general(query_head, key_head, (((1,), (1,)), ((), ())), preferred...  108 us
    dot_general x24, matrix products, attend_frame(): jnp.dot(rounded, value_head, preferred_element_type=jnp.float32) / row_total  85.3 us
    ppermute x6, waiting for transfers between devices, passed_along(): return lax.ppermute(block, axis, route)  55.7 us
    gather x6, local copies, waits for them, and re-layouts, select_tiles(): return tile_array[sources[:, None], chosen]  38.6 us
    squeeze x8, local copies, waits for them, and re-layouts, per_device(): return lax.map(attend_frame, (queries, key_set, live_slots))  34.3 us
    reduce_sum x4, other arithmetic, attend_frame(): row_total = jnp.sum(exponent, axis=1, keepdims=True)  32.2 us
    unnamed x24, local copies, waits for them, and re-layouts  26.8 us
    all_gather x1, waiting for transfers between devices, per_device(): whole_frames = lax.all_gather(paired, 'seq', axis=1, tiled=True)  18.8 us
  transfers between devices with their start and end apart: 7, of which 5 were waited for; matrix products, arithmetic and copies ran while one was open for 13% of the time, Pallas kernels for 0%

commit v1 on v0

v1 whole, which is shorter than its diff:
```python
import functools

import jax
import jax.numpy as jnp
from jax import lax
from jax.experimental import pallas as pl
from jax.experimental.pallas import tpu as pltpu
from jax.sharding import PartitionSpec as P

HEAD_DIM = 128
TILE = 128
DISTANCES = (1, 2, 4)
SCORE_SCALE = HEAD_DIM ** (-0.5) * 1.4426950408889634
GROUP = 4
ANY = pl.BlockSpec(memory_space=pl.ANY)


def list_at(lists, lengths, rank, frame, direction, entry):
    return lists[rank][(frame * 2 + direction) * lengths[rank] + entry]


def boundary_slots(lengths):
    return [
        (rank, distance, j, entry)
        for rank, distance in enumerate(DISTANCES)
        for j in range(distance)
        for entry in range(lengths[rank])
    ]


def pack_kernel(frames, frame_total, lengths, l1, l2, l4, k_own, k_other, v_own, v_other, up, down, sems):
    seq = lax.axis_index("seq")
    first = lax.axis_index("frame") * frames
    lists = (l1, l2, l4)
    half_tiles = k_own.shape[1] // TILE
    slots = boundary_slots(lengths)
    for direction, out in ((0, up), (1, down)):
        for slot, (rank, distance, j, entry) in enumerate(slots):
            if direction == 0:
                source, target = frames - distance + j, first + frames + j
            else:
                source, target = j, first - distance + j
            target = jnp.clip(target, 0, frame_total - 1)
            tile = list_at(lists, lengths, rank, target, direction, entry)
            mine = (tile // half_tiles) == seq
            rows = pl.ds(pl.multiple_of((tile % half_tiles) * TILE, TILE), TILE)
            sem = sems.at[direction * len(slots) + slot]
            for core, own, other in ((0, k_own, k_other), (1, v_own, v_other)):
                for local, ref in ((True, own), (False, other)):
                    wanted = mine if local else jnp.logical_not(mine)

                    @pl.when((seq == core) & wanted)
                    def _(ref=ref, source=source, rows=rows, out=out, slot=slot, sem=sem):
                        pltpu.make_async_copy(ref.at[source, rows, :], out.at[slot], sem).start()

    for direction, out in ((0, up), (1, down)):
        for slot in range(len(slots)):
            pltpu.make_async_copy(
                k_own.at[0, pl.ds(0, TILE), :], out.at[slot], sems.at[direction * len(slots) + slot]
            ).wait()


def scores_of(query, keys):
    return lax.dot_general(query, keys, (((1,), (1,)), ((), ())), preferred_element_type=jnp.float32)


def widened(values):
    return jnp.concatenate([values, jnp.ones_like(values)], axis=1)


def row_max(scores):
    return jnp.broadcast_to(jnp.max(scores, axis=1, keepdims=True), (scores.shape[0], HEAD_DIM))


def weights_of(scores, top):
    repeats = scores.shape[1] // HEAD_DIM
    return jnp.exp2((scores - jnp.concatenate([top] * repeats, axis=1)) * SCORE_SCALE).astype(jnp.bfloat16)


def columns(head):
    return slice(head * HEAD_DIM, (head + 1) * HEAD_DIM)


def listed_chunks(chosen, count, heads, base, q_ref, kbuf, vbuf, acc, top):
    def chunk(step, carry):
        ids = [chosen[step * GROUP + place] for place in range(GROUP)]
        spans = [pl.ds(pl.multiple_of(i * TILE, TILE), TILE) for i in ids]
        biases = [
            jnp.where(step * GROUP + place < count, jnp.float32(0.0), jnp.float32(-jnp.inf))
            for place in range(GROUP)
        ]
        all_scores = []
        for head in range(heads):
            cols = pl.ds(pl.multiple_of(base + head * HEAD_DIM, HEAD_DIM), HEAD_DIM)
            keys = jnp.concatenate([kbuf[span, cols] for span in spans], axis=0)
            scores = scores_of(q_ref[0, :, columns(head)], keys)
            parts = [scores[:, :TILE]] + [
                scores[:, place * TILE : (place + 1) * TILE] + biases[place] for place in range(1, GROUP)
            ]
            all_scores.append(jnp.concatenate(parts, axis=1))
        for head in range(heads):
            cols = pl.ds(pl.multiple_of(base + head * HEAD_DIM, HEAD_DIM), HEAD_DIM)
            values = jnp.concatenate([vbuf[span, cols] for span in spans], axis=0)
            old = top[head]
            new = jnp.maximum(old, row_max(all_scores[head]))
            factor = jnp.exp2((old - new) * SCORE_SCALE)
            weights = weights_of(all_scores[head], new)
            mixed = jnp.dot(weights, widened(values), preferred_element_type=jnp.float32)
            acc[head] = acc[head] * jnp.concatenate([factor, factor], axis=1) + mixed
            top[head] = new
        return carry

    lax.fori_loop(0, (count + GROUP - 1) // GROUP, chunk, 0)


def near_kernel(
    frames, heads, lengths, l1, l2, l4, counts, q_ref, k_own, k_other, v_own, v_other,
    acc_out, state_out, kbuf, vbuf, acc, top, chosen, sems,
):
    seq = lax.axis_index("seq")
    frame, group = pl.program_id(0), pl.program_id(1)
    half = k_own.shape[1]
    frame_tokens = 2 * half
    lists = (l1, l2, l4)

    def copies(source):
        for place, (ref, buf, owner) in enumerate(
            ((k_own, kbuf, seq), (k_other, kbuf, 1 - seq), (v_own, vbuf, seq), (v_other, vbuf, 1 - seq))
        ):
            rows = pl.ds(pl.multiple_of(source * frame_tokens + owner * half, half), half)
            yield pltpu.make_async_copy(ref.at[source], buf.at[rows, :], sems.at[source, place])

    @pl.when((frame == 0) & (group == 0))
    def _():
        for source in range(frames):
            for copy in copies(source):
                copy.start()
        for source in range(frames):
            for copy in copies(source):
                copy.wait()

    count = jnp.int32(0)
    mine = lax.axis_index("frame") * frames + frame
    for direction in (0, 1):
        for rank, distance in enumerate(DISTANCES):
            if distance >= frames:
                continue
            source = frame + (2 * direction - 1) * distance
            inside = (source >= 0) & (source < frames)
            live = counts[(mine * 2 + direction) * len(DISTANCES) + rank]
            for entry in range(lengths[rank]):
                tile = list_at(lists, lengths, rank, mine, direction, entry)
                keep = inside & (entry < live)
                chosen[count] = jnp.where(keep, source * (frame_tokens // TILE) + tile, 0)
                count = count + keep.astype(jnp.int32)
    for place in range(GROUP):
        chosen[count + place] = 0

    base = group * heads * HEAD_DIM
    rows = pl.ds(pl.multiple_of(frame * frame_tokens, frame_tokens), frame_tokens)

    def cols_of(head):
        return pl.ds(pl.multiple_of(base + head * HEAD_DIM, HEAD_DIM), HEAD_DIM)

    scores = scores_of(q_ref[0, :, columns(0)], kbuf[rows, cols_of(0)])
    for head in range(heads):
        following = None
        if head + 1 < heads:
            following = scores_of(q_ref[0, :, columns(head + 1)], kbuf[rows, cols_of(head + 1)])
        new = row_max(scores)
        acc[head] = jnp.dot(
            weights_of(scores, new), widened(vbuf[rows, cols_of(head)]), preferred_element_type=jnp.float32
        )
        top[head] = new
        scores = following
    listed_chunks(chosen, count, heads, base, q_ref, kbuf, vbuf, acc, top)
    lane = lax.broadcasted_iota(jnp.int32, (half, HEAD_DIM), 1)
    state = jnp.zeros((half, HEAD_DIM), jnp.float32)
    for head in range(heads):
        acc_out[0, :, columns(head)] = acc[head, :, :HEAD_DIM]
        state = jnp.where(lane == 2 * head, top[head], state)
        state = jnp.where(lane == 2 * head + 1, acc[head, :, HEAD_DIM:], state)
    state_out[0, 0] = state


def far_kernel(
    frames, heads, lengths, counts, q_ref, acc_in, state_in, up_own, up_other, down_own, down_other,
    out_ref, kbuf, vbuf, acc, top, chosen, sems,
):
    seq = lax.axis_index("seq")
    frame, group = pl.program_id(0), pl.program_id(1)
    rows = up_own.shape[0]
    half = q_ref.shape[1]
    slots = boundary_slots(lengths)

    def copies(core):
        for place, (own, other) in enumerate(((up_own, up_other), (down_own, down_other))):
            keys, values = (own, other) if core == 0 else (other, own)
            span = pl.ds(place * rows, rows)
            yield pltpu.make_async_copy(keys, kbuf.at[span, :], sems.at[2 * place])
            yield pltpu.make_async_copy(values, vbuf.at[span, :], sems.at[2 * place + 1])

    for core in (0, 1):

        @pl.when((frame == 0) & (group == 0) & (seq == core))
        def _(core=core):
            for copy in copies(core):
                copy.start()
            for copy in copies(core):
                copy.wait()

    count = jnp.int32(0)
    mine = lax.axis_index("frame") * frames + frame
    for direction in (0, 1):
        start = direction * len(slots)
        for rank, distance in enumerate(DISTANCES):
            place = frame if direction == 0 else frame - (frames - distance)
            crosses = (place >= 0) & (place < distance)
            live = counts[(mine * 2 + direction) * len(DISTANCES) + rank]
            for entry in range(lengths[rank]):
                keep = crosses & (entry < live)
                chosen[count] = jnp.where(keep, start + place * lengths[rank] + entry, 0)
                count = count + keep.astype(jnp.int32)
            start += distance * lengths[rank]
    for place in range(GROUP):
        chosen[count + place] = 0

    state = state_in[0, 0]
    for head in range(heads):
        acc[head, :, :HEAD_DIM] = acc_in[0, :, columns(head)]
        acc[head, :, HEAD_DIM:] = jnp.broadcast_to(state[:, 2 * head + 1 : 2 * head + 2], (half, HEAD_DIM))
        top[head] = jnp.broadcast_to(state[:, 2 * head : 2 * head + 1], (half, HEAD_DIM))
    listed_chunks(chosen, count, heads, group * heads * HEAD_DIM, q_ref, kbuf, vbuf, acc, top)
    for head in range(heads):
        out_ref[0, :, columns(head)] = (acc[head, :, :HEAD_DIM] / acc[head, :, HEAD_DIM:]).astype(jnp.bfloat16)


def per_device(queries, key_rows, value_rows, list_one, list_two, list_four, tile_counts):
    frames, half, width = queries.shape
    frame_total = list_one.shape[0]
    lengths = (list_one.shape[2], list_two.shape[2], list_four.shape[2])
    head_total = width // HEAD_DIM
    heads = max(h for h in (1, 2, 3) if head_total % h == 0)
    groups = head_total // heads
    slots = len(boundary_slots(lengths))
    lists = tuple(x.reshape(-1) for x in (list_one, list_two, list_four))
    counts = tile_counts.reshape(-1)
    listed = 2 * sum(lengths)
    devices = lax.axis_size("frame")
    swap = [(0, 1), (1, 0)]

    k_other = lax.ppermute(key_rows, "seq", swap)
    v_other = lax.ppermute(value_rows, "seq", swap)

    packed = jax.ShapeDtypeStruct((slots, TILE, width), jnp.bfloat16)
    whole = pl.BlockSpec(memory_space=pltpu.VMEM)
    up, down = pl.pallas_call(
        functools.partial(pack_kernel, frames, frame_total, lengths),
        out_shape=(packed, packed),
        in_specs=[pl.BlockSpec(memory_space=pltpu.SMEM)] * 3 + [ANY] * 4,
        out_specs=(whole, whole),
        scratch_shapes=[pltpu.SemaphoreType.DMA((2 * slots,))],
        name="pack",
    )(*lists, key_rows, k_other, value_rows, v_other)

    up = lax.ppermute(up, "frame", [(i, i + 1) for i in range(devices - 1)])
    down = lax.ppermute(down, "frame", [(i + 1, i) for i in range(devices - 1)])
    up = up.reshape(slots * TILE, width)
    down = down.reshape(slots * TILE, width)
    up_other = lax.ppermute(up, "seq", swap)
    down_other = lax.ppermute(down, "seq", swap)

    def cost(tokens):
        return pl.CostEstimate(
            flops=8 * frames * half * width * tokens,
            transcendentals=frames * half * head_total * tokens,
            bytes_accessed=40 * frames * half * width,
        )

    def block(f, g, *_):
        return (f, 0, g)

    q_spec = pl.BlockSpec((1, half, heads * HEAD_DIM), block)
    state_spec = pl.BlockSpec((1, 1, half, HEAD_DIM), lambda f, g, *_: (f, g, 0, 0))
    running = [
        pltpu.VMEM((heads, half, 2 * HEAD_DIM), jnp.float32),
        pltpu.VMEM((heads, half, HEAD_DIM), jnp.float32),
        pltpu.SMEM((listed + GROUP,), jnp.int32),
    ]
    params = pltpu.CompilerParams(vmem_limit_bytes=60 << 20)
    acc, state = pl.pallas_call(
        functools.partial(near_kernel, frames, heads, lengths),
        grid_spec=pltpu.PrefetchScalarGridSpec(
            num_scalar_prefetch=4,
            grid=(frames, groups),
            in_specs=[q_spec] + [ANY] * 4,
            out_specs=(q_spec, state_spec),
            scratch_shapes=[pltpu.VMEM((frames * 2 * half, width), jnp.bfloat16)] * 2
            + running
            + [pltpu.SemaphoreType.DMA((frames, 4))],
        ),
        out_shape=(
            jax.ShapeDtypeStruct(queries.shape, jnp.float32),
            jax.ShapeDtypeStruct((frames, groups, half, HEAD_DIM), jnp.float32),
        ),
        compiler_params=params,
        cost_estimate=cost(2 * half + listed * TILE // 2),
        name="near",
    )(*lists, counts, queries, key_rows, k_other, value_rows, v_other)

    return pl.pallas_call(
        functools.partial(far_kernel, frames, heads, lengths),
        grid_spec=pltpu.PrefetchScalarGridSpec(
            num_scalar_prefetch=1,
            grid=(frames, groups),
            in_specs=[q_spec, q_spec, state_spec] + [ANY] * 4,
            out_specs=q_spec,
            scratch_shapes=[pltpu.VMEM((2 * slots * TILE, width), jnp.bfloat16)] * 2
            + running
            + [pltpu.SemaphoreType.DMA((4,))],
        ),
        out_shape=jax.ShapeDtypeStruct(queries.shape, jnp.bfloat16),
        compiler_params=params,
        cost_estimate=cost(listed * TILE // 2),
        name="far",
    )(counts, queries, acc, state, up, up_other, down, down_other)


def solution(mesh):
    placed = P(("clips", "frame"), "seq", "head")
    listing = P("clips", None, None)
    return jax.shard_map(
        per_device,
        mesh=mesh,
        in_specs=(placed, placed, placed, listing, listing, listing, listing),
        out_specs=placed,
        check_vma=False,
    )
```

time: 479 us -> 150 us (0.31); the launches traced: 473 us -> 150 us
  matrix products: 194 us -> 0 us
  local copies, waits for them, and re-layouts: 130 us -> 4.97 us
  Pallas kernels: 0 us -> 79.2 us
  other arithmetic: 46.9 us -> 0 us
  waiting for transfers between devices: 74.6 us -> 57.7 us
  between operations: 13.6 us -> 0.07 us
  starting transfers between devices: 14.4 us -> 8.06 us
    dot_general x48 -> x0, matrix products: 194 us -> none  [the longest x24 108 us: attend_frame(): lax.dot_general(query_head, key_head, (((1,), (1,)), ((), ())), preferred...]
    pallas_call x0 -> x3, Pallas kernels: none -> 79.2 us  [the longest x1 49.2 us: per_device(): pl.pallas_call(functools.partial(near_kernel, frames, heads, lengths), gr...]
    gather x15 -> x0, local copies, waits for them, and re-layouts: 42.7 us -> none  [the longest x6 38.6 us: select_tiles(): return tile_array[sources[:, None], chosen]]
    squeeze x8 -> x0, local copies, waits for them, and re-layouts: 34.3 us -> none  [per_device(): return lax.map(attend_frame, (queries, key_set, live_slots))]
    reduce_sum x4 -> x0, other arithmetic: 32.2 us -> none  [attend_frame(): row_total = jnp.sum(exponent, axis=1, keepdims=True)]
    unnamed x24 -> x10, local copies, waits for them, and re-layouts: 26.8 us -> 2.4 us
    all_gather x1 -> x0, waiting for transfers between devices: 18.8 us -> none  [per_device(): whole_frames = lax.all_gather(paired, 'seq', axis=1, tiled=True)]
    slice x10 -> x0, local copies, waits for them, and re-layouts: 15.1 us -> none  [the longest x1 4.76 us: join_lists(): packed[0, distance][:frames_here - distance]]
  transfers between devices with their start and end apart: 7 -> 6, of which waited for: 5 -> 4; matrix products, arithmetic and copies ran while one was open for 13% -> 3% of each run, Pallas kernels for 0% -> 33%
where the time goes in v1:
time: 150 us
  Pallas kernels  79.2 us (53%)
  waiting for transfers between devices  57.7 us (38%)
  starting transfers between devices  8.06 us (5%)
  local copies, waits for them, and re-layouts  4.97 us (3%)
    pallas_call x1, Pallas kernels, per_device(): pl.pallas_call(functools.partial(near_kernel, frames, heads, lengths), gr...  49.2 us
    ppermute x1, waiting for transfers between devices, per_device(): up = lax.ppermute(up, 'frame', [(i, i + 1) for i in range(devices - 1)])  49.1 us
    pallas_call x1, Pallas kernels, per_device(): pl.pallas_call(functools.partial(far_kernel, frames, heads, lengths), gri...  24.5 us
    pallas_call x1, Pallas kernels, per_device(): pl.pallas_call(functools.partial(pack_kernel, frames, frame_total, length...  5.5 us
    ppermute x1, waiting for transfers between devices, per_device(): v_other = lax.ppermute(value_rows, 'seq', swap)  4.63 us
    ppermute x1, starting transfers between devices, per_device(): up = lax.ppermute(up, 'frame', [(i, i + 1) for i in range(devices - 1)])  3.35 us
  transfers between devices with their start and end apart: 6, of which 4 were waited for; matrix products, arithmetic and copies ran while one was open for 3% of the time, Pallas kernels for 33%

profile of v1, /device:TPU:7, one launch (start us, length us, event | category | flops | bytes accessed | tf_op | source)
XLA Modules:
  0.0 149.9 jit_solution(6337574840373308776)
XLA Ops:
  0.0 0.7 collective-permute-start
  0.7 0.0 collective-permute-start.1
  0.7 0.8 copy.15
  1.4 0.7 reshape.21.l4
  2.1 0.8 copy.13
  2.9 0.6 reshape.19.l1
  3.5 0.8 copy.14
  4.2 0.7 reshape.20.l2
  5.0 1.2 collective-permute-done.k_other
  6.2 4.6 %collective-permute-done.1.v_other = bf16[4,512,768]{2,1,0:T(8,128)(2,1)} collective-permute-done((bf16[4,512,768]{2,1,0:T(8,128)(2,1)}, bf16[4,512,768]{2,1,0:T(8,128)(2,1)}, u32[]{:S(2)}, u32[]{:S(2)}) %collective-permute-start.1) | collective-permute-done | bytes 3145760 | tf_op jit(solution)/shard_map/ppermute | solution.py:253
  10.8 5.5 %pack.1 = (bf16[12,128,768]{2,1,0:T(8,128)(2,1)}, bf16[12,128,768]{2,1,0:T(8,128)(2,1)}) custom-call(s32[128]{0:T(128)} %reshape.19.l1, s32[64]{0:T(128)} %reshape.20.l2, s32[32]{0:T(128)} %reshape.21.l4, bf16[4,512,768]{2,1,0:T(8,128)(2,1)} %k_own.3, bf16[4,512,768]{2,1,0:T(8,128)(2,1)} %copy-done, bf16[4,512,768]{2,1,0:T(8,128)(2,1)} %v_own.3, ...), custom_call_target="tpu_custom_call" | custom-call | tf_op jit(solution)/shard_map/pack/pallas_call | solution.py:257
  16.3 3.4 %collective-permute-start.2 = (bf16[12,128,768]{2,1,0:T(8,128)(2,1)}, bf16[12,128,768]{2,1,0:T(8,128)(2,1)S(1)}, u32[]{:S(2)}, u32[]{:S(2)}) collective-permute-start(bf16[12,128,768]{2,1,0:T(8,128)(2,1)} %get-tuple-element.11), channel_id=1, source_target_pairs={{0,4},{4,8},{8,12},{1,5},{5,9},{9,13},{2,6},{6,10},{10,14},{3,7},{... | collective-permute-start | bytes 7077896 | tf_op jit(solution)/shard_map/ppermute | solution.py:266
  19.7 1.3 collective-permute-start.4
  21.0 49.1 %collective-permute-done.2 = bf16[12,128,768]{2,1,0:T(8,128)(2,1)S(1)} collective-permute-done((bf16[12,128,768]{2,1,0:T(8,128)(2,1)}, bf16[12,128,768]{2,1,0:T(8,128)(2,1)S(1)}, u32[]{:S(2)}, u32[]{:S(2)}) %collective-permute-start.2) | collective-permute-done | bytes 2359328 | tf_op jit(solution)/shard_map/ppermute | solution.py:266
  70.1 1.2 collective-permute-start.3
  71.3 2.8 %collective-permute-done.4 = bf16[12,128,768]{2,1,0:T(8,128)(2,1)} collective-permute-done((bf16[12,128,768]{2,1,0:T(8,128)(2,1)}, bf16[12,128,768]{2,1,0:T(8,128)(2,1)}, u32[]{:S(2)}, u32[]{:S(2)}) %collective-permute-start.4) | collective-permute-done | bytes 2359328 | tf_op jit(solution)/shard_map/ppermute | solution.py:267
  74.0 1.5 %collective-permute-start.5 = (bf16[1536,768]{1,0:T(8,128)(2,1)}, bf16[1536,768]{1,0:T(8,128)(2,1)}, u32[]{:S(2)}, u32[]{:S(2)}) collective-permute-start(bf16[1536,768]{1,0:T(8,128)(2,1)} %bitcast.1.down_own), channel_id=1, source_target_pairs={{0,1},{1,0},{2,3},{3,2},{4,5},{5,4},{6,7},{7,6},{8,9},{9,8},{10,11... | collective-permute-start | bytes 7077896 | tf_op jit(solution)/shard_map/ppermute | solution.py:271
  75.5 0.0 copy-done.1
  75.5 0.1 copy.12
  75.6 0.6 reshape.18.counts
  76.2 49.2 %near.1 = (f32[4,512,768]{2,1,0:T(8,128)}, f32[4,2,512,128]{3,2,1,0:T(8,128)}) custom-call(s32[128]{0:T(128)} %reshape.19.l1, s32[64]{0:T(128)} %reshape.20.l2, s32[32]{0:T(128)} %reshape.21.l4, s32[96]{0:T(128)} %reshape.18.counts, bf16[4,512,768]{2,1,0:T(8,128)(2,1)} %q_ref.3, bf16[4,512,768]{2,1,0:T(8,128)(2,1)} %k_own.3, bf16[4,512,768]{2,1,0:T(8,128)(2,1)} %copy-done, ...), custom_call_target="tpu_custom_call" | custom-call | flops 24159191040 | bytes 62914560 | tf_op jit(solution)/shard_map/near/pallas_call | solution.py:291
  125.4 0.0 collective-permute-done.3.up_other
  125.4 0.0 collective-permute-done.5.down_other
  125.5 24.5 %far.1 = bf16[4,512,768]{2,1,0:T(8,128)(2,1)} custom-call(s32[96]{0:T(128)} %reshape.18.counts, bf16[4,512,768]{2,1,0:T(8,128)(2,1)} %q_ref.3, f32[4,512,768]{2,1,0:T(8,128)} %get-tuple-element.9.acc_in, f32[4,2,512,128]{3,2,1,0:T(8,128)} %get-tuple-element.10.state_in, bf16[1536,768]{1,0:T(8,128)(2,1)} %bitcast.5, ...), custom_call_target="tpu_custom_call" | custom-call | flops 11274289152 | bytes 62914560 | tf_op jit(solution)/shard_map/far/pallas_call | solution.py:311
  (5 shorter events, 0.0 us)
Async XLA Ops:
  0.0 6.2 %collective-permute-start = (bf16[4,512,768]{2,1,0:T(8,128)(2,1)}, bf16[4,512,768]{2,1,0:T(8,128)(2,1)S(1)}, u32[]{:S(2)}, u32[]{:S(2)}) collective-permute-start(bf16[4,512,768]{2,1,0:T(8,128)(2,1)} %k_own.3), channel_id=1, source_target_pairs={{0,1},{1,0},{2,3},{3,2},{4,5},{5,4},{6,7},{7,6},{8,9},{9,8},{10,11... | collective-permute-start | bytes 9437192 | tf_op jit(solution)/shard_map/ppermute | solution.py:252
  0.7 10.1 %collective-permute-start.1 = (bf16[4,512,768]{2,1,0:T(8,128)(2,1)}, bf16[4,512,768]{2,1,0:T(8,128)(2,1)}, u32[]{:S(2)}, u32[]{:S(2)}) collective-permute-start(bf16[4,512,768]{2,1,0:T(8,128)(2,1)} %v_own.3), channel_id=1, source_target_pairs={{0,1},{1,0},{2,3},{3,2},{4,5},{5,4},{6,7},{7,6},{8,9},{9,8},{10,11... | collective-permute-start | bytes 9437192 | tf_op jit(solution)/shard_map/ppermute | solution.py:253
  5.0 70.6 %copy-start.1 = (s32[16,2,3]{0,1,2:T(2,128)S(1)}, s32[16,2,3]{0,1,2:T(2,128)}, u32[]{:S(2)}) copy-start(s32[16,2,3]{0,1,2:T(2,128)} %param.13) | copy-start | bytes 1156
  6.2 4.6 %copy-start = (bf16[4,512,768]{2,1,0:T(8,128)(2,1)}, bf16[4,512,768]{2,1,0:T(8,128)(2,1)S(1)}, u32[]{:S(2)}) copy-start(bf16[4,512,768]{2,1,0:T(8,128)(2,1)S(1)} %collective-permute-done.k_other) | copy-start | bytes 9437188
  16.3 53.7 %collective-permute-start.2 = (bf16[12,128,768]{2,1,0:T(8,128)(2,1)}, bf16[12,128,768]{2,1,0:T(8,128)(2,1)S(1)}, u32[]{:S(2)}, u32[]{:S(2)}) collective-permute-start(bf16[12,128,768]{2,1,0:T(8,128)(2,1)} %get-tuple-element.11), channel_id=1, source_target_pairs={{0,4},{4,8},{8,12},{1,5},{5,9},{9,13},{2,6},{6,10},{10,14},{3,7},{... | collective-permute-start | bytes 7077896 | tf_op jit(solution)/shard_map/ppermute | solution.py:266
  19.7 54.4 %collective-permute-start.4 = (bf16[12,128,768]{2,1,0:T(8,128)(2,1)}, bf16[12,128,768]{2,1,0:T(8,128)(2,1)}, u32[]{:S(2)}, u32[]{:S(2)}) collective-permute-start(bf16[12,128,768]{2,1,0:T(8,128)(2,1)} %get-tuple-element.12), channel_id=1, source_target_pairs={{4,0},{8,4},{12,8},{5,1},{9,5},{13,9},{6,2},{10,6},{14,10},{7,3},{... | collective-permute-start | bytes 7077896 | tf_op jit(solution)/shard_map/ppermute | solution.py:267
  70.0 55.4 %copy-start.2 = (bf16[12,128,768]{2,1,0:T(8,128)(2,1)}, bf16[12,128,768]{2,1,0:T(8,128)(2,1)S(1)}, u32[]{:S(2)}) copy-start(bf16[12,128,768]{2,1,0:T(8,128)(2,1)S(1)} %collective-permute-done.2) | copy-start | bytes 7077892
  70.1 55.4 %collective-permute-start.3 = (bf16[1536,768]{1,0:T(8,128)(2,1)S(1)}, bf16[1536,768]{1,0:T(8,128)(2,1)}, u32[]{:S(2)}, u32[]{:S(2)}) collective-permute-start(bf16[1536,768]{1,0:T(8,128)(2,1)S(1)} %bitcast.4), channel_id=1, source_target_pairs={{0,1},{1,0},{2,3},{3,2},{4,5},{5,4},{6,7},{7,6},{8,9},{9,8},{10,11... | collective-permute-start | bytes 7077896 | tf_op jit(solution)/shard_map/ppermute | solution.py:270
  74.0 51.4 %collective-permute-start.5 = (bf16[1536,768]{1,0:T(8,128)(2,1)}, bf16[1536,768]{1,0:T(8,128)(2,1)}, u32[]{:S(2)}, u32[]{:S(2)}) collective-permute-start(bf16[1536,768]{1,0:T(8,128)(2,1)} %bitcast.1.down_own), channel_id=1, source_target_pairs={{0,1},{1,0},{2,3},{3,2},{4,5},{5,4},{6,7},{7,6},{8,9},{9,8},{10,11... | collective-permute-start | bytes 7077896 | tf_op jit(solution)/shard_map/ppermute | solution.py:271
